TPU v7x, 512 devices: a whole 4x4x16 slice. The times are simulated.
512 devices in a mesh: mp: 2 (over y_hi), tok: 8 (over x, core), lat: 32 (over z, y_lo).
Axes of the slice: x: 4, y: 4 (y_hi: 2, y_lo: 2; y = y_hi * 2 + y_lo), z: 16, core: 2. Of those that a mesh axis runs over, the one named last changes fastest.
Arguments:
- inputs: bfloat16 [2, 384, 4608], P('mp', 'lat', 'tok'), may hold values from -6 to 6
- gate_w: bfloat16 [2, 4608, 18432], P('mp', 'tok', 'lat'), may hold values from -0.09375 to 0.09375
- up_w: bfloat16 [2, 4608, 18432], P('mp', 'tok', 'lat'), may hold values from -0.09375 to 0.09375
- down_w: bfloat16 [2, 18432, 4608], P('mp', 'lat', 'tok'), may hold values from -0.046875 to 0.046875
- enc_w: bfloat16 [2, 4608, 8192], P('mp', 'tok', 'lat'), may hold values from -0.0625 to 0.0625
- enc_bias: float32 [8192], P('lat'), may hold values from -3 to 3
- dec_w: bfloat16 [8192, 2, 4608], P('lat', 'mp', 'tok'), may hold values from -0.0625 to 0.0625
- dec_bias: float32 [2, 4608], P('mp', 'tok'), may hold values from -3 to 3
Outputs:
- recon_error: float32 [2, 384, 4608], P('mp', 'lat', 'tok')
- dec_grad: float32 [8192, 2, 4608], P('lat', 'mp', 'tok')
- latent_grad: float32 [384, 8192], P(None, 'lat')
All inputs are finite; a program needn't handle non-finite values.
Results may differ from a plain program's by a relative error of at most 0.009.
Values may be sent and summed in bfloat16 or wider, within the bound.
A program may use at most 64 MiB of HBM per device.

v0:
```python
import itertools

import jax
import jax.numpy as jnp
from jax import lax
from jax.experimental import pallas as pl
from jax.experimental.pallas import tpu as pltpu
from jax.sharding import PartitionSpec as P

MESH = pl.DeviceIdType.MESH
F32, BF16 = jnp.float32, jnp.bfloat16
GELU = 0.7978845608028654


def dot(a, b, ca=1, cb=0):
    return lax.dot_general(a, b, (((ca,), (cb,)), ((), ())), preferred_element_type=F32)


def gelu(v):
    return 0.5 * v * (1.0 + jnp.tanh(GELU * (v + 0.044715 * v * v * v)))


def kernel(
    x_hbm, gate_hbm, up_hbm, down_hbm, enc_hbm, ebias_hbm, dect_hbm, dbias_hbm,
    err_ref, gradt_ref, lat_ref,
    x_ref, gate_ref, up_ref, down_ref, enc_ref, ebias_ref, dect_ref, dbias_ref,
    xpair, xall,
    part, bcore, bsum, brecv, hid,
    dpart, dnear, dsum, dfar, acts,
    gpart, gnear, gsum, gfar, err,
    fpart, frecv, codes, ipart, irecv, lgrad,
    ssem, rsem, lsem,
):
    mp, tok, lat = lax.axis_index("mp"), lax.axis_index("tok"), lax.axis_index("lat")
    z, yl = lat // 2, lat % 2
    r, k = z % 4, z // 4
    xc, core = tok // 2, tok % 2
    q = mp * 8 + tok

    def at_z(d, y=None):
        return (mp, tok, ((z + d + 16) % 16) * 2 + (yl if y is None else y))

    def at_x(d):
        return (mp, ((xc + d) % 4) * 2 + core, lat)

    def at_q(d):
        o = (q + d) % 16
        return (o // 8, o % 8, lat)

    y_mate = (mp, tok, z * 2 + 1 - yl)
    core_mate = (mp, xc * 2 + 1 - core, lat)

    barrier = pltpu.get_barrier_semaphore()
    peers = [at_z(d) for d in (8, 4, 12)] + [at_z(d, y) for d in (2, -2, 1, -1) for y in range(2)]
    peers += [y_mate] + [at_q(d) for d in range(1, 16)]
    for peer in peers:
        pl.semaphore_signal(barrier, inc=1, device_id=peer, device_id_type=MESH)

    fetches = [
        pltpu.make_async_copy(src, dst, lsem.at[i])
        for i, (src, dst) in enumerate(
            (
                (x_hbm, x_ref), (gate_hbm, gate_ref), (up_hbm, up_ref), (down_hbm, down_ref),
                (enc_hbm, enc_ref), (ebias_hbm, ebias_ref), (dect_hbm, dect_ref), (dbias_hbm, dbias_ref),
            )
        )
    ]
    for fetch in fetches:
        fetch.start()

    count = [0]
    sent, awaited, landed, here = [], [], set(), set()

    def slots(n):
        count[0] += n
        return count[0] - n

    def send(src, dst, peer, out, into):
        copy = pltpu.make_async_remote_copy(
            src_ref=src, dst_ref=dst, send_sem=ssem.at[out], recv_sem=rsem.at[into], device_id=peer, device_id_type=MESH
        )
        copy.start()
        sent.append(copy)

    def coming(landing, slot):
        copy = pltpu.make_async_remote_copy(
            src_ref=landing, dst_ref=landing, send_sem=ssem.at[slot], recv_sem=rsem.at[slot], device_id=y_mate, device_id_type=MESH
        )
        awaited.append(copy)
        return copy

    def trade(src, dst, peer, landing):
        slot = slots(1)
        send(src, dst, peer, slot, slot)
        return coming(landing, slot)

    def land(copies):
        for copy in copies:
            landed.add(id(copy))
            copy.wait_recv()

    def fetched(*numbers):
        for i in numbers:
            if i not in here:
                here.add(i)
                fetches[i].wait()

    def finish():
        land([copy for copy in awaited if id(copy) not in landed])
        fetched(*range(len(fetches)))
        for copy in sent:
            copy.wait_send()

    def flat(v, width):
        return v.astype(F32).reshape(192, width).astype(BF16)

    def gather_inputs(buf):
        up1, down1, two = slots(4), slots(4), slots(4)
        far = {}
        for off in (2, 3, 1):
            c = (k + 4 - off) % 4
            own = buf.at[r, k // 2, k % 2]
            far[off] = trade(own, own, at_z(4 * off), buf.at[r, c // 2, c % 2])
        for off in (0, 3, 1, 2):
            c = (k + 4 - off) % 4
            if off:
                land([far[off]])
            piece = buf.at[r, c // 2, c % 2]
            send(piece, piece, at_z(2 - 4 * (c // 2)), two + c, two + c)
            send(piece, piece, at_z(1), up1 + c, up1 + c)
            send(piece, piece, at_z(-1), down1 + c, down1 + c)
        for c in range(4):
            land([
                coming(buf.at[(r + 3) % 4, c // 2, c % 2], up1 + c),
                coming(buf.at[(r + 1) % 4, c // 2, c % 2], down1 + c),
                coming(buf.at[(r + 2) % 4, c // 2, c % 2], two + c),
            ])

    def reduce_start(p, near, h):
        base = slots(7)
        for i, d in enumerate((-2 if h == 0 else 2, 1, -1)):
            for y in range(2):
                s = 2 * i + yl
                send(p.at[(r + d + 4) % 4, y], near.at[s], at_z(d, y), base + 2 * i + y, base + s)
        send(p.at[r, 1 - yl], near.at[6], y_mate, base + 6, base + 6)
        return [coming(near.at[s], base + s) for s in range(7)]

    def far_start(p, near, copies, total, far):
        land(copies)
        acc = p[r, yl].astype(F32)
        for s in range(7):
            acc = acc + near[s].astype(F32)
        total[...] = acc.astype(BF16)
        return [trade(total, far.at[off - 1], at_z(4 * off), far.at[off - 1]) for off in (2, 1, 3)]

    def far_sum(copies, total, far):
        land(copies)
        return total[...].astype(F32) + far[0].astype(F32) + far[1].astype(F32) + far[2].astype(F32)

    def spread_start(buf, h):
        base = slots(7)
        own = buf.at[r, yl]
        copies = []
        for i, d in enumerate((2 if h == 0 else -2, 1, -1)):
            for y in range(2):
                send(own, own, at_z(d, y), base + 2 * i + y, base + 2 * i + yl)
                copies.append(coming(buf.at[(r - d + 4) % 4, y], base + 2 * i + y))
        return copies + [trade(own, own, y_mate, buf.at[r, 1 - yl])]

    def scatter_start(p, recv):
        copies = []
        for d in range(1, 16):
            o = (q + d) % 16
            copies.append(trade(p.at[o // 8, o % 8], recv.at[d - 1], at_q(d), recv.at[d - 1]))
        return copies

    def scatter_sum(copies, p, recv):
        acc = p[mp, tok].astype(F32)
        for d, copy in enumerate(copies):
            land([copy])
            acc = acc + recv[d].astype(F32)
        return acc

    def gather_start(buf):
        own = buf.at[mp, tok]
        copies = []
        for d in range(1, 16):
            o = (q + 16 - d) % 16
            copies.append(trade(own, own, at_q(d), buf.at[o // 8, o % 8]))
        return copies

    def split(v):
        v = v.reshape(8, 24, 256)
        return v[:, :, :128].astype(BF16), v[:, :, 128:].astype(BF16)

    def join(buf):
        return jnp.concatenate([flat(buf[0], 128), flat(buf[1], 128)], axis=1)

    def chain(h):
        block = flat(xall[:, :, h], 576)
        fetched(1)
        part[h, 0] = dot(block, gate_ref[...]).reshape(4, 2, 24, 576).astype(BF16)
        cores = [trade(part.at[h, 0, :, 1 - core], bcore.at[h, 0], core_mate, bcore.at[h, 0])]
        fetched(2)
        part[h, 1] = dot(block, up_ref[...]).reshape(4, 2, 24, 576).astype(BF16)
        cores += [trade(part.at[h, 1, :, 1 - core], bcore.at[h, 1], core_mate, bcore.at[h, 1])]
        yield "b_dot"
        land(cores)
        for g in range(2):
            bsum[h, :, g] = (part[h, g, :, core].astype(F32) + bcore[h, g].astype(F32)).astype(BF16)
        across = [trade(bsum.at[h, (xc + d) % 4], brecv.at[h, d - 1], at_x(d), brecv.at[h, d - 1]) for d in (2, 1, 3)]
        yield "b_core"
        land(across)
        both = bsum[h, xc].astype(F32)
        for d in range(3):
            both = both + brecv[h, d].astype(F32)
        hid[h, xc, core] = (gelu(both[0]) * both[1]).astype(BF16)
        own = hid.at[h, xc, core]
        across = {d: trade(own, own, at_x(d), hid.at[h, (xc + 4 - d) % 4, core]) for d in (2, 1, 3)}
        cores = [trade(own, own, core_mate, hid.at[h, xc, 1 - core])]
        yield "b_x"
        for d in (1, 3, 2):
            land([across[d]])
            j = (xc + 4 - d) % 4
            cores.append(trade(hid.at[h, j, core], hid.at[h, j, core], core_mate, hid.at[h, j, 1 - core]))
        yield "c_x"
        land(cores)

        fetched(3)
        dpart[h] = dot(flat(hid[h], 576), down_ref[...]).reshape(4, 2, 24, 576).astype(BF16)
        copies = reduce_start(dpart.at[h], dnear.at[h], h)
        yield "d_dot"
        copies = far_start(dpart.at[h], dnear.at[h], copies, dsum.at[h], dfar.at[h])
        yield "d_near"
        acts[h, r, yl] = far_sum(copies, dsum.at[h], dfar.at[h]).astype(BF16)
        copies = spread_start(acts.at[h], h)
        yield "d_far"
        land(copies)

        fetched(4, 5)
        fpart[h, 0], fpart[h, 1] = split(dot(flat(acts[h], 576), enc_ref[...]))
        copies = scatter_start(fpart.at[h], frecv.at[h])
        yield "e_near"
        bias = jnp.where(mp == 0, ebias_ref[:, :128], ebias_ref[:, 128:])
        pre = scatter_sum(copies, fpart.at[h], frecv.at[h]) + bias
        codes[h, mp, tok] = jnp.maximum(pre, 0.0).astype(BF16)
        copies = gather_start(codes.at[h])
        yield "f_rs"
        land(copies)

        fetched(6, 7)
        gpart[h] = dot(join(codes[h]), dect_ref[...], 1, 1).reshape(4, 2, 24, 576).astype(BF16)
        copies = reduce_start(gpart.at[h], gnear.at[h], h)
        yield "f_ag"
        copies = far_start(gpart.at[h], gnear.at[h], copies, gsum.at[h], gfar.at[h])
        yield "g_near"
        error = far_sum(copies, gsum.at[h], gfar.at[h]) + dbias_ref[...] - acts[h, r, yl].astype(F32)
        err[h, r, yl] = error.astype(BF16)
        copies = spread_start(err.at[h], h)
        yield "g_far"
        land(copies)

        ipart[h, 0], ipart[h, 1] = split(dot(flat(err[h], 576), dect_ref[...]))
        copies = scatter_start(ipart.at[h], irecv.at[h])
        yield "h_near"
        lgrad[h, mp, tok] = scatter_sum(copies, ipart.at[h], irecv.at[h]).astype(BF16)
        copies = gather_start(lgrad.at[h])
        yield "i_rs"
        if h == 0:
            gradt_ref[...] = dot(flat(err[0], 576), join(codes[0]), 0, 0)
        else:
            gradt_ref[...] += dot(flat(err[1], 576), join(codes[1]), 0, 0)
            rows = err[k % 2, r, k // 2].astype(F32)
            err_ref[...] = jnp.where(yl == 0, rows[0:12], rows[12:24])
        yield "grad"
        land(copies)
        for c in range(2):
            for j in range(8):
                first = 24 * (4 * (2 * (j % 2) + h) + j // 2)
                lat_ref[first : first + 24, 128 * c : 128 * c + 128] = lgrad[h, c, j].astype(F32)

    fetched(0)
    pl.semaphore_wait(barrier, len(peers))

    land([trade(x_ref, xpair, y_mate, xpair)])
    mine, theirs = x_ref[...].astype(F32), xpair[...].astype(F32)
    first = jnp.where(yl == 0, mine, theirs)
    second = jnp.where(yl == 0, theirs, mine)
    xall[r, k // 2, k % 2] = jnp.concatenate([first, second], axis=0).astype(BF16)
    gather_inputs(xall)
    for at in itertools.zip_longest(chain(0), chain(1)):
        pass
    finish()


def body(inputs, gate_w, up_w, down_w, enc_w, enc_bias, dec_w, dec_bias):
    vmem = pl.BlockSpec(memory_space=pltpu.VMEM)
    reduce_scratch = [
        pltpu.VMEM((2, 4, 2, 24, 576), BF16), pltpu.VMEM((2, 7, 24, 576), BF16), pltpu.VMEM((2, 24, 576), BF16),
        pltpu.VMEM((2, 3, 24, 576), BF16), pltpu.VMEM((2, 4, 2, 24, 576), BF16),
    ]
    q_scratch = [
        pltpu.VMEM((2, 2, 8, 24, 128), BF16), pltpu.VMEM((2, 15, 24, 128), BF16), pltpu.VMEM((2, 2, 8, 24, 128), BF16)
    ]
    err, gradt, lat = pl.pallas_call(
        kernel,
        out_shape=(
            jax.ShapeDtypeStruct((12, 576), F32),
            jax.ShapeDtypeStruct((576, 256), F32),
            jax.ShapeDtypeStruct((384, 256), F32),
        ),
        in_specs=[pl.BlockSpec(memory_space=pl.ANY)] * 8,
        out_specs=(vmem, vmem, vmem),
        scratch_shapes=[
            pltpu.VMEM((12, 576), BF16), pltpu.VMEM((576, 576), BF16), pltpu.VMEM((576, 576), BF16),
            pltpu.VMEM((576, 576), BF16), pltpu.VMEM((576, 256), BF16), pltpu.VMEM((1, 256), F32),
            pltpu.VMEM((576, 256), BF16), pltpu.VMEM((1, 576), F32),
            pltpu.VMEM((12, 576), BF16), pltpu.VMEM((4, 2, 2, 24, 576), BF16),
            pltpu.VMEM((2, 2, 4, 2, 24, 576), BF16), pltpu.VMEM((2, 2, 4, 24, 576), BF16), pltpu.VMEM((2, 4, 2, 24, 576), BF16),
            pltpu.VMEM((2, 3, 2, 24, 576), BF16), pltpu.VMEM((2, 4, 2, 24, 576), BF16),
            *reduce_scratch, *reduce_scratch, *q_scratch, *q_scratch,
            pltpu.SemaphoreType.DMA((240,)), pltpu.SemaphoreType.DMA((240,)), pltpu.SemaphoreType.DMA((8,)),
        ],
        compiler_params=pltpu.CompilerParams(collective_id=0, has_side_effects=True, vmem_limit_bytes=56 << 20),
        name="step",
    )(
        inputs[0], gate_w[0], up_w[0], down_w[0], enc_w[0], enc_bias[None], dec_w[:, 0, :].T, dec_bias,
    )
    return err[None], gradt.T[:, None, :], lat


def solution(mesh):
    in_specs = (
        P("mp", "lat", "tok"),
        P("mp", "tok", "lat"),
        P("mp", "tok", "lat"),
        P("mp", "lat", "tok"),
        P("mp", "tok", "lat"),
        P("lat"),
        P("lat", "mp", "tok"),
        P("mp", "tok"),
    )
    out_specs = (P("mp", "lat", "tok"), P("lat", "mp", "tok"), P(None, "lat"))
    return jax.shard_map(body, mesh=mesh, in_specs=in_specs, out_specs=out_specs, check_vma=False)
```

profile of v0, /device:TPU:1, one launch (start us, length us, event | category | flops | bytes accessed | tf_op | source)
XLA Modules:
  0.0 130.8 jit_solution(16784069069057808378)
XLA Ops:
  0.6 126.0 %step.1 = (f32[12,576]{1,0:T(8,128)}, f32[576,256]{1,0:T(8,128)}, f32[384,256]{1,0:T(8,128)}) custom-call(bf16[12,576]{1,0:T(8,128)(2,1)} %bitcast.20, bf16[576,576]{1,0:T(8,128)(2,1)} %bitcast.13, bf16[576,576]{1,0:T(8,128)(2,1)} %bitcast.14, bf16[576,576]{1,0:T(8,128)(2,1)} %bitcast.15, bf16[576,256]{1,0:T(8,128)(2,1)} %bitcast.17, f32[1,256]{1,0:T(1,128)} %bitcast.21, ...), custom_call_target="tpu_custom_call" | custom-call | tf_op jit(solution)/shard_map/step/pallas_call | solution.py:305
  126.7 1.4 %copy.11 = f32[1,12,576]{2,0,1:T(1,128)} copy(f32[1,12,576]{2,1,0:T(8,128)} %bitcast.19) | data formatting | bytes 55296
  128.1 0.0 copy-start
  128.1 2.0 %copy.14 = f32[256,1,576]{0,2,1:T(8,128)} copy(f32[256,1,576]{0,2,1:T(8,128)} %bitcast.16) | data formatting | bytes 1179648
  130.1 0.0 copy-done
  130.1 0.7 copy.15
Async XLA Ops:
  128.1 2.0 %copy-start = (f32[384,256]{1,0:T(8,128)S(1)}, f32[384,256]{1,0:T(8,128)}, u32[]{:S(2)}) copy-start(f32[384,256]{1,0:T(8,128)} %get-tuple-element.17) | copy-start | bytes 1179652
where the time goes:
time: 131 us
  Pallas kernels  126 us (96%)
  local copies, waits for them, and re-layouts  4.14 us (3%)
    pallas_call x1, Pallas kernels, body(): pl.pallas_call(kernel, out_shape=(jax.ShapeDtypeStruct((12, 576), F32), j...  126 us
    unnamed x5, local copies, waits for them, and re-layouts  4.14 us

commit v1 on v0

--- a/solution.py
+++ b/solution.py
@@ -37,21 +37,32 @@
     xc, core = tok // 2, tok % 2
     q = mp * 8 + tok
 
-    def at_z(d, y=None):
-        return (mp, tok, ((z + d + 16) % 16) * 2 + (yl if y is None else y))
+    known = {}
+
+    def at_z(d, y):
+        if ("z", d % 16) not in known:
+            known["z", d % 16] = ((z + d + 16) % 16) * 2
+        return (mp, tok, known["z", d % 16] + y)
 
     def at_x(d):
-        return (mp, ((xc + d) % 4) * 2 + core, lat)
+        if ("x", d) not in known:
+            known["x", d] = ((xc + d) % 4) * 2 + core
+        return (mp, known["x", d], lat)
+
+    def index_q(d):
+        if ("q", d % 16) not in known:
+            o = (q + d + 16) % 16
+            known["q", d % 16] = (o // 8, o % 8)
+        return known["q", d % 16]
 
     def at_q(d):
-        o = (q + d) % 16
-        return (o // 8, o % 8, lat)
+        return (*index_q(d), lat)
 
     y_mate = (mp, tok, z * 2 + 1 - yl)
     core_mate = (mp, xc * 2 + 1 - core, lat)
 
     barrier = pltpu.get_barrier_semaphore()
-    peers = [at_z(d) for d in (8, 4, 12)] + [at_z(d, y) for d in (2, -2, 1, -1) for y in range(2)]
+    peers = [at_z(d, y) for d in (8, 4, 12, 2, -2, 1, -1) for y in range(2)]
     peers += [y_mate] + [at_q(d) for d in range(1, 16)]
     for peer in peers:
         pl.semaphore_signal(barrier, inc=1, device_id=peer, device_id_type=MESH)
@@ -120,15 +131,15 @@
         for off in (2, 3, 1):
             c = (k + 4 - off) % 4
             own = buf.at[r, k // 2, k % 2]
-            far[off] = trade(own, own, at_z(4 * off), buf.at[r, c // 2, c % 2])
+            far[off] = trade(own, own, at_z(4 * off, yl), buf.at[r, c // 2, c % 2])
         for off in (0, 3, 1, 2):
             c = (k + 4 - off) % 4
             if off:
                 land([far[off]])
             piece = buf.at[r, c // 2, c % 2]
-            send(piece, piece, at_z(2 - 4 * (c // 2)), two + c, two + c)
-            send(piece, piece, at_z(1), up1 + c, up1 + c)
-            send(piece, piece, at_z(-1), down1 + c, down1 + c)
+            send(piece, piece, (mp, tok, ((z + 18 - 4 * (c // 2)) % 16) * 2 + yl), two + c, two + c)
+            send(piece, piece, at_z(1, yl), up1 + c, up1 + c)
+            send(piece, piece, at_z(-1, yl), down1 + c, down1 + c)
         for c in range(4):
             land([
                 coming(buf.at[(r + 3) % 4, c // 2, c % 2], up1 + c),
@@ -138,10 +149,12 @@
 
     def reduce_start(p, near, h):
         base = slots(7)
-        for i, d in enumerate((-2 if h == 0 else 2, 1, -1)):
-            for y in range(2):
-                s = 2 * i + yl
-                send(p.at[(r + d + 4) % 4, y], near.at[s], at_z(d, y), base + 2 * i + y, base + s)
+        for i, step in enumerate((2, 1, -1)):
+            for o in range(2):
+                d = step if i else (2 if o == h else -2)
+                y = yl if o == 0 else 1 - yl
+                s = 2 * i + o
+                send(p.at[(r + d + 4) % 4, y], near.at[s], at_z(d, y), base + s, base + s)
         send(p.at[r, 1 - yl], near.at[6], y_mate, base + 6, base + 6)
         return [coming(near.at[s], base + s) for s in range(7)]
 
@@ -151,27 +164,29 @@
         for s in range(7):
             acc = acc + near[s].astype(F32)
         total[...] = acc.astype(BF16)
-        return [trade(total, far.at[off - 1], at_z(4 * off), far.at[off - 1]) for off in (2, 1, 3)]
+        return [trade(total, far.at[off - 1], at_z(4 * off, yl), far.at[off - 1]) for off in (2, 1, 3)]
 
     def far_sum(copies, total, far):
         land(copies)
         return total[...].astype(F32) + far[0].astype(F32) + far[1].astype(F32) + far[2].astype(F32)
 
     def spread_start(buf, h):
-        base = slots(7)
+        base = slots(6)
         own = buf.at[r, yl]
         copies = []
-        for i, d in enumerate((2 if h == 0 else -2, 1, -1)):
-            for y in range(2):
-                send(own, own, at_z(d, y), base + 2 * i + y, base + 2 * i + yl)
-                copies.append(coming(buf.at[(r - d + 4) % 4, y], base + 2 * i + y))
+        for i, step in enumerate((2, 1, -1)):
+            for o in range(2):
+                d = step if i else (-2 if o == h else 2)
+                y = yl if o == 0 else 1 - yl
+                s = base + 2 * i + o
+                send(own, own, at_z(d, y), s, s)
+                copies.append(coming(buf.at[(r - d + 4) % 4, y], s))
         return copies + [trade(own, own, y_mate, buf.at[r, 1 - yl])]
 
     def scatter_start(p, recv):
         copies = []
         for d in range(1, 16):
-            o = (q + d) % 16
-            copies.append(trade(p.at[o // 8, o % 8], recv.at[d - 1], at_q(d), recv.at[d - 1]))
+            copies.append(trade(p.at[index_q(d)], recv.at[d - 1], at_q(d), recv.at[d - 1]))
         return copies
 
     def scatter_sum(copies, p, recv):
@@ -185,8 +200,7 @@
         own = buf.at[mp, tok]
         copies = []
         for d in range(1, 16):
-            o = (q + 16 - d) % 16
-            copies.append(trade(own, own, at_q(d), buf.at[o // 8, o % 8]))
+            copies.append(trade(own, own, at_q(d), buf.at[index_q(-d)]))
         return copies
 
     def split(v):
@@ -223,7 +237,6 @@
             land([across[d]])
             j = (xc + 4 - d) % 4
             cores.append(trade(hid.at[h, j, core], hid.at[h, j, core], core_mate, hid.at[h, j, 1 - core]))
-        yield "c_x"
         land(cores)
 
         fetched(3)
@@ -302,6 +315,7 @@
     q_scratch = [
         pltpu.VMEM((2, 2, 8, 24, 128), BF16), pltpu.VMEM((2, 15, 24, 128), BF16), pltpu.VMEM((2, 2, 8, 24, 128), BF16)
     ]
+    operands = (inputs[0], gate_w[0], up_w[0], down_w[0], enc_w[0], enc_bias[None], dec_w[:, 0, :].T, dec_bias)
     err, gradt, lat = pl.pallas_call(
         kernel,
         out_shape=(
@@ -312,8 +326,8 @@
         in_specs=[pl.BlockSpec(memory_space=pl.ANY)] * 8,
         out_specs=(vmem, vmem, vmem),
         scratch_shapes=[
-            pltpu.VMEM((12, 576), BF16), pltpu.VMEM((576, 576), BF16), pltpu.VMEM((576, 576), BF16),
-            pltpu.VMEM((576, 576), BF16), pltpu.VMEM((576, 256), BF16), pltpu.VMEM((1, 256), F32),
+            pltpu.VMEM((12, 576), BF16), pltpu.VMEM((576, 576), BF16), pltpu.VMEM((576, 576), BF16), pltpu.VMEM((576, 576), BF16),
+            pltpu.VMEM((576, 256), BF16), pltpu.VMEM((1, 256), F32),
             pltpu.VMEM((576, 256), BF16), pltpu.VMEM((1, 576), F32),
             pltpu.VMEM((12, 576), BF16), pltpu.VMEM((4, 2, 2, 24, 576), BF16),
             pltpu.VMEM((2, 2, 4, 2, 24, 576), BF16), pltpu.VMEM((2, 2, 4, 24, 576), BF16), pltpu.VMEM((2, 4, 2, 24, 576), BF16),
@@ -321,10 +335,10 @@
             *reduce_scratch, *reduce_scratch, *q_scratch, *q_scratch,
             pltpu.SemaphoreType.DMA((240,)), pltpu.SemaphoreType.DMA((240,)), pltpu.SemaphoreType.DMA((8,)),
         ],
-        compiler_params=pltpu.CompilerParams(collective_id=0, has_side_effects=True, vmem_limit_bytes=56 << 20),
+        compiler_params=pltpu.CompilerParams(collective_id=0, has_side_effects=True, vmem_limit_bytes=40 << 20),
         name="step",
     )(
-        inputs[0], gate_w[0], up_w[0], down_w[0], enc_w[0], enc_bias[None], dec_w[:, 0, :].T, dec_bias,
+        *(pltpu.with_memory_space_constraint(v, pltpu.HBM) for v in operands)
     )
     return err[None], gradt.T[:, None, :], lat
 

time: 131 us -> 128 us (0.977)
  local copies, waits for them, and re-layouts: 4.14 us -> 2.2 us
    unnamed x5 -> x3, local copies, waits for them, and re-layouts: 4.14 us -> 2.2 us
where the time goes in v1:
time: 128 us
  Pallas kernels  125 us (98%)
  local copies, waits for them, and re-layouts  2.2 us (2%)
    pallas_call x1, Pallas kernels, body(): pl.pallas_call(kernel, out_shape=(jax.ShapeDtypeStruct((12, 576), F32), j...  125 us

profile of v1, /device:TPU:1, one launch (start us, length us, event | category | flops | bytes accessed | tf_op | source)
XLA Modules:
  0.0 128.3 jit_solution(9000075347351996091)
XLA Ops:
  0.6 125.5 %step.1 = (f32[12,576]{1,0:T(8,128)S(1)}, f32[576,256]{1,0:T(8,128)S(1)}, f32[384,256]{1,0:T(8,128)S(1)}) custom-call(bf16[12,576]{1,0:T(8,128)(2,1)} %bitcast.20, bf16[576,576]{1,0:T(8,128)(2,1)} %bitcast.15, bf16[576,576]{1,0:T(8,128)(2,1)} %bitcast.16, bf16[576,576]{1,0:T(8,128)(2,1)} %bitcast.17, bf16[576,256]{1,0:T(8,128)(2,1)} %bitcast.18, ...), custom_call_target="tpu_custom_call" | custom-call | tf_op jit(solution)/shard_map/step/pallas_call | solution.py:319
  126.1 0.6 copy.11
  126.8 0.8 copy.14
  127.6 0.7 copy.15

commit v2 on v1

--- a/solution.py
+++ b/solution.py
@@ -23,8 +23,8 @@
 def kernel(
     x_hbm, gate_hbm, up_hbm, down_hbm, enc_hbm, ebias_hbm, dect_hbm, dbias_hbm,
     err_ref, gradt_ref, lat_ref,
-    x_ref, gate_ref, up_ref, down_ref, enc_ref, ebias_ref, dect_ref, dbias_ref,
-    xpair, xall,
+    gate_ref, up_ref, down_ref, enc_ref, ebias_ref, dect_ref, dbias_ref,
+    xall,
     part, bcore, bsum, brecv, hid,
     dpart, dnear, dsum, dfar, acts,
     gpart, gnear, gsum, gfar, err,
@@ -62,7 +62,7 @@
     core_mate = (mp, xc * 2 + 1 - core, lat)
 
     barrier = pltpu.get_barrier_semaphore()
-    peers = [at_z(d, y) for d in (8, 4, 12, 2, -2, 1, -1) for y in range(2)]
+    peers = [at_z(d, y) for d in (4, -4, 2, -2, 1, -1) for y in range(2)]
     peers += [y_mate] + [at_q(d) for d in range(1, 16)]
     for peer in peers:
         pl.semaphore_signal(barrier, inc=1, device_id=peer, device_id_type=MESH)
@@ -71,7 +71,7 @@
         pltpu.make_async_copy(src, dst, lsem.at[i])
         for i, (src, dst) in enumerate(
             (
-                (x_hbm, x_ref), (gate_hbm, gate_ref), (up_hbm, up_ref), (down_hbm, down_ref),
+                (x_hbm, xall.at[r, k // 2, k % 2, yl]), (gate_hbm, gate_ref), (up_hbm, up_ref), (down_hbm, down_ref),
                 (enc_hbm, enc_ref), (ebias_hbm, ebias_ref), (dect_hbm, dect_ref), (dbias_hbm, dbias_ref),
             )
         )
@@ -126,20 +126,34 @@
         return v.astype(F32).reshape(192, width).astype(BF16)
 
     def gather_inputs(buf):
-        up1, down1, two = slots(4), slots(4), slots(4)
-        far = {}
-        for off in (2, 3, 1):
+        base, up1, down1, two = slots(7), slots(4), slots(4), slots(4)
+        own = buf.at[r, k // 2, k % 2, yl]
+
+        def chunk(off):
             c = (k + 4 - off) % 4
-            own = buf.at[r, k // 2, k % 2]
-            far[off] = trade(own, own, at_z(4 * off, yl), buf.at[r, c // 2, c % 2])
-        for off in (0, 3, 1, 2):
-            c = (k + 4 - off) % 4
-            if off:
-                land([far[off]])
-            piece = buf.at[r, c // 2, c % 2]
+            return c, buf.at[r, c // 2, c % 2]
+
+        def pass_on(off):
+            c, piece = chunk(off)
             send(piece, piece, (mp, tok, ((z + 18 - 4 * (c // 2)) % 16) * 2 + yl), two + c, two + c)
             send(piece, piece, at_z(1, yl), up1 + c, up1 + c)
             send(piece, piece, at_z(-1, yl), down1 + c, down1 + c)
+
+        for i, d in enumerate((4, -4)):
+            for y in range(2):
+                send(own, own, at_z(d, y), base + 2 * i + y, base + 2 * i + yl)
+        send(own, own, y_mate, base + 4, base + 4)
+        for i, off in enumerate((1, 3)):
+            land([coming(chunk(off)[1].at[y], base + 2 * i + y) for y in range(2)])
+        c = (k + 3 + 2 * core) % 4
+        relay = buf.at[r, c // 2, c % 2]
+        send(relay, relay, (mp, tok, ((z + 20 - 8 * core) % 16) * 2 + yl), base + 5, base + 5)
+        land([coming(chunk(0)[1].at[1 - yl], base + 4)])
+        pass_on(0)
+        pass_on(1)
+        pass_on(3)
+        land([coming(chunk(2)[1], base + 5)])
+        pass_on(2)
         for c in range(4):
             land([
                 coming(buf.at[(r + 3) % 4, c // 2, c % 2], up1 + c),
@@ -211,7 +225,10 @@
         return jnp.concatenate([flat(buf[0], 128), flat(buf[1], 128)], axis=1)
 
     def chain(h):
-        block = flat(xall[:, :, h], 576)
+        pieces = [
+            jnp.concatenate([xall[i // 2, i % 2, h, y].astype(F32) for y in range(2)], axis=0) for i in range(8)
+        ]
+        block = jnp.concatenate(pieces, axis=0).astype(BF16)
         fetched(1)
         part[h, 0] = dot(block, gate_ref[...]).reshape(4, 2, 24, 576).astype(BF16)
         cores = [trade(part.at[h, 0, :, 1 - core], bcore.at[h, 0], core_mate, bcore.at[h, 0])]
@@ -295,11 +312,6 @@
     fetched(0)
     pl.semaphore_wait(barrier, len(peers))
 
-    land([trade(x_ref, xpair, y_mate, xpair)])
-    mine, theirs = x_ref[...].astype(F32), xpair[...].astype(F32)
-    first = jnp.where(yl == 0, mine, theirs)
-    second = jnp.where(yl == 0, theirs, mine)
-    xall[r, k // 2, k % 2] = jnp.concatenate([first, second], axis=0).astype(BF16)
     gather_inputs(xall)
     for at in itertools.zip_longest(chain(0), chain(1)):
         pass
@@ -326,10 +338,10 @@
         in_specs=[pl.BlockSpec(memory_space=pl.ANY)] * 8,
         out_specs=(vmem, vmem, vmem),
         scratch_shapes=[
-            pltpu.VMEM((12, 576), BF16), pltpu.VMEM((576, 576), BF16), pltpu.VMEM((576, 576), BF16), pltpu.VMEM((576, 576), BF16),
+            pltpu.VMEM((576, 576), BF16), pltpu.VMEM((576, 576), BF16), pltpu.VMEM((576, 576), BF16),
             pltpu.VMEM((576, 256), BF16), pltpu.VMEM((1, 256), F32),
             pltpu.VMEM((576, 256), BF16), pltpu.VMEM((1, 576), F32),
-            pltpu.VMEM((12, 576), BF16), pltpu.VMEM((4, 2, 2, 24, 576), BF16),
+            pltpu.VMEM((4, 2, 2, 2, 12, 576), BF16),
             pltpu.VMEM((2, 2, 4, 2, 24, 576), BF16), pltpu.VMEM((2, 2, 4, 24, 576), BF16), pltpu.VMEM((2, 4, 2, 24, 576), BF16),
             pltpu.VMEM((2, 3, 2, 24, 576), BF16), pltpu.VMEM((2, 4, 2, 24, 576), BF16),
             *reduce_scratch, *reduce_scratch, *q_scratch, *q_scratch,

time: 128 us -> 128 us (level)
  no operation moved by 1% of the time
where the time goes in v2:
time: 128 us
  Pallas kernels  125 us (98%)
  local copies, waits for them, and re-layouts  2.2 us (2%)
    pallas_call x1, Pallas kernels, body(): pl.pallas_call(kernel, out_shape=(jax.ShapeDtypeStruct((12, 576), F32), j...  125 us

profile of v2, /device:TPU:1, one launch (start us, length us, event | category | flops | bytes accessed | tf_op | source)
XLA Modules:
  0.0 127.7 jit_solution(1974645860071281537)
XLA Ops:
  0.6 124.8 %step.1 = (f32[12,576]{1,0:T(8,128)S(1)}, f32[576,256]{1,0:T(8,128)S(1)}, f32[384,256]{1,0:T(8,128)S(1)}) custom-call(bf16[12,576]{1,0:T(8,128)(2,1)} %bitcast.20, bf16[576,576]{1,0:T(8,128)(2,1)} %bitcast.15, bf16[576,576]{1,0:T(8,128)(2,1)} %bitcast.16, bf16[576,576]{1,0:T(8,128)(2,1)} %bitcast.17, bf16[576,256]{1,0:T(8,128)(2,1)} %bitcast.18, ...), custom_call_target="tpu_custom_call" | custom-call | tf_op jit(solution)/shard_map/step/pallas_call | solution.py:331
  125.5 0.6 copy.11
  126.1 0.8 copy.14
  126.9 0.7 copy.15

commit v3 on v2

--- a/solution.py
+++ b/solution.py
@@ -49,21 +49,20 @@
             known["x", d] = ((xc + d) % 4) * 2 + core
         return (mp, known["x", d], lat)
 
-    def index_q(d):
-        if ("q", d % 16) not in known:
-            o = (q + d + 16) % 16
-            known["q", d % 16] = (o // 8, o % 8)
-        return known["q", d % 16]
-
-    def at_q(d):
-        return (*index_q(d), lat)
+    def index_q(a, d, c):
+        if ("q", a, d % 4, c) not in known:
+            known["q", a, d % 4, c] = (1 - mp if a else mp, ((xc + d + 4) % 4) * 2 + (1 - core if c else core))
+        return known["q", a, d % 4, c]
+
+    others = [(a, d, c) for a, d in ((1, 2), (1, 1), (1, 3), (0, 2), (1, 0), (0, 1), (0, 3), (0, 0)) for c in range(2)][:-2]
+    others.append((0, 0, 1))
 
     y_mate = (mp, tok, z * 2 + 1 - yl)
     core_mate = (mp, xc * 2 + 1 - core, lat)
 
     barrier = pltpu.get_barrier_semaphore()
     peers = [at_z(d, y) for d in (4, -4, 2, -2, 1, -1) for y in range(2)]
-    peers += [y_mate] + [at_q(d) for d in range(1, 16)]
+    peers += [y_mate] + [(*index_q(*o), lat) for o in others]
     for peer in peers:
         pl.semaphore_signal(barrier, inc=1, device_id=peer, device_id_type=MESH)
 
@@ -198,24 +197,20 @@
         return copies + [trade(own, own, y_mate, buf.at[r, 1 - yl])]
 
     def scatter_start(p, recv):
-        copies = []
-        for d in range(1, 16):
-            copies.append(trade(p.at[index_q(d)], recv.at[d - 1], at_q(d), recv.at[d - 1]))
-        return copies
+        return [
+            trade(p.at[index_q(*o)], recv.at[i], (*index_q(*o), lat), recv.at[i]) for i, o in enumerate(others)
+        ]
 
     def scatter_sum(copies, p, recv):
         acc = p[mp, tok].astype(F32)
-        for d, copy in enumerate(copies):
-            land([copy])
-            acc = acc + recv[d].astype(F32)
+        for i in reversed(range(15)):
+            land([copies[i]])
+            acc = acc + recv[i].astype(F32)
         return acc
 
     def gather_start(buf):
         own = buf.at[mp, tok]
-        copies = []
-        for d in range(1, 16):
-            copies.append(trade(own, own, at_q(d), buf.at[index_q(-d)]))
-        return copies
+        return [trade(own, own, (*index_q(*o), lat), buf.at[index_q(o[0], -o[1], o[2])]) for o in others]
 
     def split(v):
         v = v.reshape(8, 24, 256)
@@ -301,7 +296,7 @@
         else:
             gradt_ref[...] += dot(flat(err[1], 576), join(codes[1]), 0, 0)
             rows = err[k % 2, r, k // 2].astype(F32)
-            err_ref[...] = jnp.where(yl == 0, rows[0:12], rows[12:24])
+            err_ref[...] = jnp.where(yl == 0, rows[0:12], rows[12:24]).reshape(12, 1, 576)
         yield "grad"
         land(copies)
         for c in range(2):
@@ -316,6 +311,15 @@
     for at in itertools.zip_longest(chain(0), chain(1)):
         pass
     finish()
+
+
+def store(err_ref, gradt_ref, lat_ref, err_hbm, gradt_hbm, lat_hbm, sems):
+    pairs = ((gradt_ref, gradt_hbm), (lat_ref, lat_hbm), (err_ref, err_hbm))
+    copies = [pltpu.make_async_copy(src, dst, sems.at[i]) for i, (src, dst) in enumerate(pairs)]
+    for copy in copies:
+        copy.start()
+    for copy in copies:
+        copy.wait()
 
 
 def body(inputs, gate_w, up_w, down_w, enc_w, enc_bias, dec_w, dec_bias):
@@ -331,7 +335,7 @@
     err, gradt, lat = pl.pallas_call(
         kernel,
         out_shape=(
-            jax.ShapeDtypeStruct((12, 576), F32),
+            jax.ShapeDtypeStruct((12, 1, 576), F32),
             jax.ShapeDtypeStruct((576, 256), F32),
             jax.ShapeDtypeStruct((384, 256), F32),
         ),
@@ -352,7 +356,21 @@
     )(
         *(pltpu.with_memory_space_constraint(v, pltpu.HBM) for v in operands)
     )
-    return err[None], gradt.T[:, None, :], lat
+    hbm = pl.BlockSpec(memory_space=pl.ANY)
+    err, gradt, lat = pl.pallas_call(
+        store,
+        out_shape=(
+            jax.ShapeDtypeStruct((12, 1, 576), F32),
+            jax.ShapeDtypeStruct((576, 256), F32),
+            jax.ShapeDtypeStruct((384, 256), F32),
+        ),
+        in_specs=[hbm] * 3,
+        out_specs=(hbm, hbm, hbm),
+        scratch_shapes=[pltpu.SemaphoreType.DMA((3,))],
+        compiler_params=pltpu.CompilerParams(vmem_limit_bytes=4 << 20),
+        name="store",
+    )(err, gradt, lat)
+    return jnp.transpose(err, (1, 0, 2)), gradt.T[:, None, :], lat
 
 
 def solution(mesh):

time: 128 us -> 123 us (0.961)
  Pallas kernels: 125 us -> 122 us
  local copies, waits for them, and re-layouts: 2.2 us -> 0 us
    pallas_call x1 -> x2, Pallas kernels: 125 us -> 122 us  [the longest x1 121 us: body(): pl.pallas_call(kernel, out_shape=(jax.ShapeDtypeStruct((12, 1, 576), F32)...]
    unnamed x3 -> x0, local copies, waits for them, and re-layouts: 2.2 us -> none
where the time goes in v3:
time: 123 us
  Pallas kernels  122 us (99%)
    pallas_call x1, Pallas kernels, body(): pl.pallas_call(kernel, out_shape=(jax.ShapeDtypeStruct((12, 1, 576), F32)...  121 us

profile of v3, /device:TPU:1, one launch (start us, length us, event | category | flops | bytes accessed | tf_op | source)
XLA Modules:
  0.0 122.8 jit_solution(7783363837397001436)
XLA Ops:
  0.6 121.2 %step.1 = (f32[12,1,576]{2,1,0:T(1,128)S(1)}, f32[576,256]{1,0:T(8,128)S(1)}, f32[384,256]{1,0:T(8,128)S(1)}) custom-call(bf16[12,576]{1,0:T(8,128)(2,1)} %bitcast.18, bf16[576,576]{1,0:T(8,128)(2,1)} %bitcast.13, bf16[576,576]{1,0:T(8,128)(2,1)} %bitcast.14, bf16[576,576]{1,0:T(8,128)(2,1)} %bitcast.15, bf16[576,256]{1,0:T(8,128)(2,1)} %bitcast.16, ...), custom_call_target="tpu_custom_call" | custom-call | tf_op jit(solution)/shard_map/step/pallas_call | solution.py:335
  121.9 1.0 store.1
